TPU v7x, 32 devices: a whole 2x2x4 slice. The times are simulated.
32 devices in a mesh: cluster: 2 (over x), sub: 16 (over z, y, core).
Axes of the slice: x: 2, y: 2, z: 4, core: 2. Of those that a mesh axis runs over, the one named last changes fastest.
Arguments:
- load_terms: float32 [32, 128, 1536], P(('cluster', 'sub')), may hold values from -60 to 60
- dual_operator: bfloat16 [32, 1536, 1536], P(('cluster', 'sub')), may hold values from -2 to 16, as said below
- dirichlet: bfloat16 [32, 1536, 1536], P(('cluster', 'sub')), may hold values from -2 to 16, as said below
- corner_coupling: bfloat16 [32, 1536, 24], P(('cluster', 'sub')), may hold values from -0.25 to 0.25
- coarse_inverse: float32 [96, 96], P(('cluster', 'sub')), may hold values from -2 to 4, as said below
- face_map: int32 [32, 6, 256], P(('cluster', 'sub')), may hold values from 0 to 255, as said below
- face_live: int32 [32, 6], P(('cluster', 'sub')), may hold values from 0 to 1, as said below
- corner_ids: int32 [32, 8], P(('cluster', 'sub')), may hold values from 0 to 31, as said below
Outputs:
- multipliers: float32 [32, 128, 1536], P(('cluster', 'sub'))
- residual: float32 [32, 128, 1536], P(('cluster', 'sub'))
Inputs may be any that keep to these rules, and one draw needn't show every extreme that they name: face_map[d, f] is a permutation of the slots of a face; the maps of the two sides of a face pair are inverse to each other. `face_live`: equal on the two sides of a face pair. `corner_ids`: the eight corners of a subdomain are the lattice vertices (c + a, s + b + 4 * e) for a, b, e in 0 and 1, taken modulo 2 and 16; each vertex has one number and is shared by eight subdomains. `dual_operator`: each subdomain's matrix is symmetric and positive definite. `dirichlet`: each subdomain's matrix is symmetric and positive definite. `coarse_inverse`: symmetric and positive definite.
All inputs are finite; a program needn't handle non-finite values.
Results may differ from a plain program's by a relative error of at most 0.0099.
Values sent between devices are 32-bit elements; how exact they have to be, the bound alone decides.
No kernel may reach another device: no remote copies, remote signals or barrier semaphores. Data moves between devices by JAX's collectives and lax.ppermute only.
A program may use at most 128 MiB of HBM per device.

v0:
```python
import jax
import jax.numpy as jnp
from jax import lax
from jax.sharding import PartitionSpec as P

ITERS = 2
STRIDE = 4


def padded(block, sides, width):
    for axis, dim in sides:
        count = lax.axis_size(axis)
        forward = [(i, i + 1) for i in range(count - 1)]
        forward.append((count - 1, 0))
        backward = [(target, source) for source, target in forward]
        low = lax.ppermute(
            lax.slice_in_dim(block, block.shape[dim] - width, None, axis=dim), axis, forward
        )
        high = lax.ppermute(lax.slice_in_dim(block, 0, width, axis=dim), axis, backward)
        block = jnp.concatenate([low, block, high], axis=dim)
    return block


def passed_along(value, axis, steps):
    count = lax.axis_size(axis)
    pairs = [(source, (source + steps) % count) for source in range(count)]
    return lax.ppermute(value, axis, pairs)


def local(
    load_terms,
    dual_operator,
    dirichlet,
    corner_coupling,
    coarse_inverse,
    face_map,
    face_live,
    corner_ids,
):
    local_loads = load_terms[0]
    operator_local = dual_operator[0]
    precond_local = dirichlet[0]
    coupling = corner_coupling[0]
    slot_maps = face_map[0]
    live_faces = face_live[0].astype(jnp.float32)
    corners = corner_ids[0]
    load_count = local_loads.shape[0]
    dual_size = local_loads.shape[1]
    face_size = dual_size // 6
    coarse_size = coarse_inverse.shape[1]
    coarse_index = (3 * corners[:, None] + jnp.arange(3, dtype=jnp.int32)[None, :]).reshape(-1)
    spread = (coarse_index[:, None] == jnp.arange(coarse_size, dtype=jnp.int32)[None, :]).astype(
        jnp.float32
    )

    def assemble(local_sum):
        face_parts = local_sum.reshape(load_count, 6, face_size)
        slab_pair = padded(jnp.stack([face_parts[:, 0], face_parts[:, 1]]), (("cluster", 0),), 1)
        row_pair = padded(jnp.stack([face_parts[:, 2], face_parts[:, 3]]), (("sub", 0),), 1)
        column_pair = []
        for source_face, shift_step in ((5, STRIDE), (4, -STRIDE)):
            column_pair.append(passed_along(face_parts[:, source_face], "sub", shift_step))
        received = [
            slab_pair[0],
            slab_pair[3],
            row_pair[0],
            row_pair[3],
            column_pair[0],
            column_pair[1],
        ]
        pieces = []
        for face_index in range(6):
            permuted = jnp.take(received[face_index], slot_maps[face_index], axis=1)
            pieces.append((face_parts[:, face_index] + permuted) * live_faces[face_index])
        return jnp.concatenate(pieces, axis=1)

    def precond_with_product(vector):
        local_term = jnp.dot(
            vector.astype(jnp.bfloat16), precond_local, preferred_element_type=jnp.float32
        )
        precond = assemble(local_term)
        product = 0.5 * lax.psum(jnp.sum(vector * precond, axis=1), ("cluster", "sub"))
        return (precond, product)

    right_side = assemble(local_loads)
    multipliers = jnp.zeros_like(right_side)
    residual = right_side
    precond, residual_dot = precond_with_product(residual)
    direction = precond
    for iteration in range(ITERS):
        rounded = direction.astype(jnp.bfloat16)
        direct = jnp.dot(rounded, operator_local, preferred_element_type=jnp.float32)
        corner_terms = jnp.dot(rounded, coupling, preferred_element_type=jnp.float32)
        coarse_local = jnp.dot(corner_terms, spread, precision=lax.Precision.HIGHEST)
        local_curve = jnp.sum(direction * direct, axis=1)
        apply_coarse_load, curve_total = lax.psum((coarse_local, local_curve), ("cluster", "sub"))
        own_values = jnp.dot(apply_coarse_load, coarse_inverse.T, precision=lax.Precision.HIGHEST)
        solution = lax.all_gather(own_values, ("cluster", "sub"), axis=1, tiled=True)
        corner_values = jnp.dot(solution, spread.T, precision=lax.Precision.HIGHEST).astype(
            jnp.bfloat16
        )
        back = lax.dot_general(
            corner_values, coupling, (((1,), (1,)), ((), ())), preferred_element_type=jnp.float32
        )
        dual_image = assemble(direct + back)
        curvature = curve_total + jnp.sum(apply_coarse_load * solution, axis=1)
        dual_image, curvature = (dual_image, curvature)
        step_size = residual_dot / curvature
        multipliers = multipliers + step_size[:, None] * direction
        residual = residual - step_size[:, None] * dual_image
        if iteration + 1 < ITERS:
            precond, residual_new = precond_with_product(residual)
            direction = precond + (residual_new / residual_dot)[:, None] * direction
            residual_dot = residual_new
    return (multipliers[None], residual[None])


def solution(mesh):
    placed = (
        P(("cluster", "sub"), None, None),
        P(("cluster", "sub"), None, None),
        P(("cluster", "sub"), None, None),
        P(("cluster", "sub"), None, None),
        P(("cluster", "sub"), None),
        P(("cluster", "sub"), None, None),
        P(("cluster", "sub"), None),
        P(("cluster", "sub"), None),
    )
    return jax.shard_map(
        local,
        mesh=mesh,
        in_specs=placed,
        out_specs=(P(("cluster", "sub"), None, None), P(("cluster", "sub"), None, None)),
        check_vma=False,
    )
```

profile of v0, /device:TPU:0, one launch (start us, length us, event | category | flops | bytes accessed | tf_op | source)
XLA Modules:
  0.0 432.1 jit_solution(1258101771140866283)
XLA Ops:
  2.3 3.0 collective-permute-start
  5.8 4.5 %collective-permute-start.3 = (f32[1,128,256]{2,1,0:T(8,128)S(1)}, f32[1,128,256]{2,1,0:T(8,128)S(1)}, u32[]{:S(2)}, u32[]{:S(2)}) collective-permute-start(f32[1,128,256]{2,1,0:T(8,128)S(1)} %bitcast.561), channel_id=1, source_target_pairs={{1,0},{2,1},{3,2},{4,3},{5,4},{6,5},{7,6},{8,7},{9,8},{10,9},{11,1... | collective-permute-start | bytes 393224 | tf_op jit(solution)/shard_map/ppermute | solution.py:19
  12.5 3.6 collective-permute-start.5
  16.1 6.6 %copy.173 = bf16[1,1536,1536]{1,2,0:T(8,128)(2,1)} copy(bf16[1,1536,1536]{2,1,0:T(8,128)(2,1)} %param.12) | data formatting | bytes 9437184 | tf_op args[2]
  33.2 4.0 fusion.6
  37.3 2.1 collective-permute-start.6
  39.4 4.4 %collective-permute-start.9 = (f32[1,128,256]{2,1,0:T(8,128)S(1)}, f32[1,128,256]{2,1,0:T(8,128)S(1)}, u32[]{:S(2)}, u32[]{:S(2)}) collective-permute-start(f32[1,128,256]{2,1,0:T(8,128)S(1)} %get-tuple-element.30), channel_id=1, source_target_pairs={{1,0},{2,1},{3,2},{4,3},{5,4},{6,5},{7,6},{8,7},{9,8},{10,9},{11,1... | collective-permute-start | bytes 393224 | tf_op jit(solution)/shard_map/ppermute | solution.py:19
  44.0 3.9 collective-permute-start.11
  60.1 3.8 multiply_reduce_fusion.3
  65.1 37.5 %all-reduce.1 = (f32[128,96]{0,1:T(8,128)S(1)}, f32[128]{0:T(128)}, f32[128]{0:T(128)}) all-reduce(f32[128,96]{0,1:T(8,128)} %fusion.53, f32[128]{0:T(128)} %get-tuple-element.4, f32[128]{0:T(128)} %get-tuple-element.3), channel_id=1, replica_groups=mesh['cluster'=2,'sub'=16] {'cluster','sub'}, use_global_device_ids=true, to_apply=%region_4.6 | all-reduce | flops 12544 | bytes 100352 | tf_op jit(solution)/shard_map/psum | solution.py:96
  103.4 41.8 %all-gather = f32[32,3,128]{2,1,0:T(4,128)S(1)} all-gather(f32[1,3,128]{2,1,0:T(4,128)S(1)} %convolution_bitcast_fusion.1), channel_id=1, replica_groups=mesh['cluster'=2,'sub'=16] {'cluster','sub'}, dimensions={0}, use_global_device_ids=true | all-gather | bytes 50688 | tf_op jit(solution)/shard_map/all_gather | solution.py:98
  152.3 2.0 collective-permute-start.13
  155.5 4.5 %collective-permute-start.15 = (f32[1,128,256]{2,1,0:T(8,128)S(1)}, f32[1,128,256]{2,1,0:T(8,128)}, u32[]{:S(2)}, u32[]{:S(2)}) collective-permute-start(f32[1,128,256]{2,1,0:T(8,128)S(1)} %bitcast.568), channel_id=1, source_target_pairs={{1,0},{2,1},{3,2},{4,3},{5,4},{6,5},{7,6},{8,7},{9,8},{10,9},{11,1... | collective-permute-start | bytes 393224 | tf_op jit(solution)/shard_map/ppermute | solution.py:19
  162.1 4.0 collective-permute-start.17
  172.5 1.7 copy.192
  176.6 1.7 copy.196
  180.6 1.7 copy.198
  185.6 2.3 constant_dynamic-update-slice_fusion.17
  191.3 2.2 constant_dynamic-update-slice_fusion.16
  193.5 2.3 constant_dynamic-update-slice_fusion.15
  195.7 2.1 constant_dynamic-update-slice_fusion.14
  200.6 4.3 fusion.4
  205.8 1.9 collective-permute-start.19
  207.7 4.4 %collective-permute-start.21 = (f32[1,128,256]{2,1,0:T(8,128)}, f32[1,128,256]{2,1,0:T(8,128)}, u32[]{:S(2)}, u32[]{:S(2)}) collective-permute-start(f32[1,128,256]{2,1,0:T(8,128)} %get-tuple-element.18), channel_id=1, source_target_pairs={{1,0},{2,1},{3,2},{4,3},{5,4},{6,5},{7,6},{8,7},{9,8},{10,9},{11,1... | collective-permute-start | bytes 393224 | tf_op jit(solution)/shard_map/ppermute | solution.py:19
  212.2 3.8 collective-permute-start.23
  218.4 1.7 copy.206
  222.4 1.7 copy.208
  226.4 1.7 copy.210
  230.4 1.7 copy.212
  236.1 2.2 constant_dynamic-update-slice_fusion.23
  241.6 2.2 constant_dynamic-update-slice_fusion.22
  243.8 2.2 constant_dynamic-update-slice_fusion.21
  246.1 2.1 constant_dynamic-update-slice_fusion.20
  248.2 2.2 constant_dynamic-update-slice_fusion.19
  251.8 1.7 multiply_reduce_fusion.1
  253.5 36.9 %psum.45 = f32[128]{0:T(128)S(1)} all-reduce(f32[128]{0:T(128)S(1)} %multiply_reduce_fusion.1), channel_id=1, replica_groups=mesh['cluster'=2,'sub'=16] {'cluster','sub'}, use_global_device_ids=true, to_apply=%region_7.9 | all-reduce | flops 128 | bytes 1024 | tf_op jit(solution)/shard_map/psum | solution.py:82
  292.4 4.3 multiply_reduce_fusion
  297.0 41.7 %all-reduce = (f32[128]{0:T(128)}, f32[128,96]{0,1:T(8,128)S(1)}) all-reduce(f32[128]{0:T(128)} %get-tuple-element.85, f32[128,96]{0,1:T(8,128)S(1)} %fusion.52), channel_id=1, replica_groups=mesh['cluster'=2,'sub'=16] {'cluster','sub'}, use_global_device_ids=true, to_apply=%region_9.11 | all-reduce | flops 12416 | bytes 99328 | tf_op jit(solution)/shard_map/psum | solution.py:96
  338.8 41.1 %all-gather.1 = f32[32,3,128]{2,1,0:T(4,128)S(1)} all-gather(f32[1,3,128]{2,1,0:T(4,128)S(1)} %convolution_bitcast_fusion), channel_id=1, replica_groups=mesh['cluster'=2,'sub'=16] {'cluster','sub'}, dimensions={0}, use_global_device_ids=true | all-gather | bytes 50688 | tf_op jit(solution)/shard_map/all_gather | solution.py:98
  384.5 1.9 collective-permute-start.25
  388.5 4.5 %collective-permute-start.27 = (f32[1,128,256]{2,1,0:T(8,128)S(1)}, f32[1,128,256]{2,1,0:T(8,128)}, u32[]{:S(2)}, u32[]{:S(2)}) collective-permute-start(f32[1,128,256]{2,1,0:T(8,128)S(1)} %bitcast.573), channel_id=1, source_target_pairs={{1,0},{2,1},{3,2},{4,3},{5,4},{6,5},{7,6},{8,7},{9,8},{10,9},{11,1... | collective-permute-start | bytes 393224 | tf_op jit(solution)/shard_map/ppermute | solution.py:19
  395.5 3.8 collective-permute-start.29
  414.4 1.7 copy.235
  416.1 2.8 bitcast_dynamic-update-slice_fusion.10
  418.9 2.7 bitcast_dynamic-update-slice_fusion.9
  421.7 2.6 bitcast_dynamic-update-slice_fusion.8
  424.3 2.4 bitcast_dynamic-update-slice_fusion.7
  428.3 3.8 multiply_subtract_fusion
  (373 shorter events, 106.2 us)
Async XLA Ops:
  0.6 63.3 %copy-start = (bf16[1,1536,24]{1,2,0:T(8,128)(2,1)S(1)}, bf16[1,1536,24]{1,2,0:T(8,128)(2,1)}, u32[]{:S(2)}) copy-start(bf16[1,1536,24]{1,2,0:T(8,128)(2,1)} %param.13) | copy-start | bytes 221188
  2.3 10.2 %collective-permute-start = (f32[1,128,256]{2,1,0:T(8,128)S(1)}, f32[1,128,256]{2,1,0:T(8,128)S(1)}, u32[]{:S(2)}, u32[]{:S(2)}) collective-permute-start(f32[1,128,256]{2,1,0:T(8,128)S(1)} %bitcast.563), channel_id=1, source_target_pairs={{0,16},{16,0},{1,17},{17,1},{2,18},{18,2},{3,19},{19,3},{4,20},{20... | collective-permute-start | bytes 393224 | tf_op jit(solution)/shard_map/ppermute | solution.py:16
  5.4 18.9 %collective-permute-start.1 = (f32[1,128,256]{2,1,0:T(8,128)S(1)}, f32[1,128,256]{2,1,0:T(8,128)S(1)}, u32[]{:S(2)}, u32[]{:S(2)}) collective-permute-start(f32[1,128,256]{2,1,0:T(8,128)S(1)} %bitcast.564), channel_id=1, source_target_pairs={{16,0},{0,16},{17,1},{1,17},{18,2},{2,18},{19,3},{3,19},{20,4},{4,... | collective-permute-start | bytes 393224 | tf_op jit(solution)/shard_map/ppermute | solution.py:19
  5.6 19.7 %collective-permute-start.2 = (f32[1,128,256]{2,1,0:T(8,128)S(1)}, f32[1,128,256]{2,1,0:T(8,128)S(1)}, u32[]{:S(2)}, u32[]{:S(2)}) collective-permute-start(f32[1,128,256]{2,1,0:T(8,128)S(1)} %bitcast.560), channel_id=1, source_target_pairs={{0,1},{1,2},{2,3},{3,4},{4,5},{5,6},{6,7},{7,8},{8,9},{9,10},{10,1... | collective-permute-start | bytes 393224 | tf_op jit(solution)/shard_map/ppermute | solution.py:16
  5.8 20.5 %collective-permute-start.3 = (f32[1,128,256]{2,1,0:T(8,128)S(1)}, f32[1,128,256]{2,1,0:T(8,128)S(1)}, u32[]{:S(2)}, u32[]{:S(2)}) collective-permute-start(f32[1,128,256]{2,1,0:T(8,128)S(1)} %bitcast.561), channel_id=1, source_target_pairs={{1,0},{2,1},{3,2},{4,3},{5,4},{6,5},{7,6},{8,7},{9,8},{10,9},{11,1... | collective-permute-start | bytes 393224 | tf_op jit(solution)/shard_map/ppermute | solution.py:19
  10.4 16.9 %collective-permute-start.4 = (f32[128,256]{1,0:T(8,128)S(1)}, f32[128,256]{1,0:T(8,128)S(1)}, u32[]{:S(2)}, u32[]{:S(2)}) collective-permute-start(f32[128,256]{1,0:T(8,128)S(1)} %bitcast.559), channel_id=1, source_target_pairs={{0,4},{1,5},{2,6},{3,7},{4,8},{5,9},{6,10},{7,11},{8,12},{9,13},{1... | collective-permute-start | bytes 393224 | tf_op jit(solution)/shard_map/ppermute | solution.py:27
  11.5 41.2 %copy-start.70 = (pred[256]{0:T(512)(128)(4,1)}, pred[256]{0:T(512)(128)(4,1)S(1)}, u32[]{:S(2)}) copy-start(pred[256]{0:T(512)(128)(4,1)S(1)} %compare_and_fusion.5) | copy-start | bytes 772
  11.5 45.2 %copy-start.68 = (pred[256]{0:T(512)(128)(4,1)}, pred[256]{0:T(512)(128)(4,1)S(1)}, u32[]{:S(2)}) copy-start(pred[256]{0:T(512)(128)(4,1)S(1)} %compare_and_fusion.4) | copy-start | bytes 772
  11.6 45.8 %copy-start.66 = (pred[256]{0:T(512)(128)(4,1)}, pred[256]{0:T(512)(128)(4,1)S(1)}, u32[]{:S(2)}) copy-start(pred[256]{0:T(512)(128)(4,1)S(1)} %compare_and_fusion.3) | copy-start | bytes 772
  11.6 46.5 %copy-start.64 = (pred[256]{0:T(512)(128)(4,1)}, pred[256]{0:T(512)(128)(4,1)S(1)}, u32[]{:S(2)}) copy-start(pred[256]{0:T(512)(128)(4,1)S(1)} %compare_and_fusion.2) | copy-start | bytes 772
  11.6 47.0 %copy-start.62 = (pred[256]{0:T(512)(128)(4,1)}, pred[256]{0:T(512)(128)(4,1)S(1)}, u32[]{:S(2)}) copy-start(pred[256]{0:T(512)(128)(4,1)S(1)} %compare_and_fusion.1) | copy-start | bytes 772
  11.7 47.7 %copy-start.60 = (pred[256]{0:T(512)(128)(4,1)}, pred[256]{0:T(512)(128)(4,1)S(1)}, u32[]{:S(2)}) copy-start(pred[256]{0:T(512)(128)(4,1)S(1)} %compare_and_fusion) | copy-start | bytes 772
  12.5 15.7 %collective-permute-start.5 = (f32[128,256]{1,0:T(8,128)S(1)}, f32[128,256]{1,0:T(8,128)S(1)}, u32[]{:S(2)}, u32[]{:S(2)}) collective-permute-start(f32[128,256]{1,0:T(8,128)S(1)} %bitcast.562), channel_id=1, source_target_pairs={{0,12},{1,13},{2,14},{3,15},{4,0},{5,1},{6,2},{7,3},{8,4},{9,5},{1... | collective-permute-start | bytes 393224 | tf_op jit(solution)/shard_map/ppermute | solution.py:27
  37.3 6.8 %collective-permute-start.6 = (f32[1,128,256]{2,1,0:T(8,128)S(1)}, f32[1,128,256]{2,1,0:T(8,128)S(1)}, u32[]{:S(2)}, u32[]{:S(2)}) collective-permute-start(f32[1,128,256]{2,1,0:T(8,128)S(1)} %get-tuple-element.33), channel_id=1, source_target_pairs={{0,16},{16,0},{1,17},{17,1},{2,18},{18,2},{3,19},{19,3},{4,20},{20... | collective-permute-start | bytes 393224 | tf_op jit(solution)/shard_map/ppermute | solution.py:16
  39.3 9.5 %collective-permute-start.7 = (f32[1,128,256]{2,1,0:T(8,128)S(1)}, f32[1,128,256]{2,1,0:T(8,128)S(1)}, u32[]{:S(2)}, u32[]{:S(2)}) collective-permute-start(f32[1,128,256]{2,1,0:T(8,128)S(1)} %get-tuple-element.29), channel_id=1, source_target_pairs={{16,0},{0,16},{17,1},{1,17},{18,2},{2,18},{19,3},{3,19},{20,4},{4,... | collective-permute-start | bytes 393224 | tf_op jit(solution)/shard_map/ppermute | solution.py:19
  39.4 10.4 %collective-permute-start.8 = (f32[1,128,256]{2,1,0:T(8,128)S(1)}, f32[1,128,256]{2,1,0:T(8,128)S(1)}, u32[]{:S(2)}, u32[]{:S(2)}) collective-permute-start(f32[1,128,256]{2,1,0:T(8,128)S(1)} %get-tuple-element.32), channel_id=1, source_target_pairs={{0,1},{1,2},{2,3},{3,4},{4,5},{5,6},{6,7},{7,8},{8,9},{9,10},{10,1... | collective-permute-start | bytes 393224 | tf_op jit(solution)/shard_map/ppermute | solution.py:16
  39.4 11.3 %collective-permute-start.9 = (f32[1,128,256]{2,1,0:T(8,128)S(1)}, f32[1,128,256]{2,1,0:T(8,128)S(1)}, u32[]{:S(2)}, u32[]{:S(2)}) collective-permute-start(f32[1,128,256]{2,1,0:T(8,128)S(1)} %get-tuple-element.30), channel_id=1, source_target_pairs={{1,0},{2,1},{3,2},{4,3},{5,4},{6,5},{7,6},{8,7},{9,8},{10,9},{11,1... | collective-permute-start | bytes 393224 | tf_op jit(solution)/shard_map/ppermute | solution.py:19
  43.9 7.8 %collective-permute-start.10 = (f32[128,256]{1,0:T(8,128)S(1)}, f32[128,256]{1,0:T(8,128)S(1)}, u32[]{:S(2)}, u32[]{:S(2)}) collective-permute-start(f32[128,256]{1,0:T(8,128)S(1)} %get-tuple-element.31), channel_id=1, source_target_pairs={{0,4},{1,5},{2,6},{3,7},{4,8},{5,9},{6,10},{7,11},{8,12},{9,13},{1... | collective-permute-start | bytes 393224 | tf_op jit(solution)/shard_map/ppermute | solution.py:27
  44.0 9.3 %collective-permute-start.11 = (f32[128,256]{1,0:T(8,128)S(1)}, f32[128,256]{1,0:T(8,128)}, u32[]{:S(2)}, u32[]{:S(2)}) collective-permute-start(f32[128,256]{1,0:T(8,128)S(1)} %get-tuple-element.28), channel_id=1, source_target_pairs={{0,12},{1,13},{2,14},{3,15},{4,0},{5,1},{6,2},{7,3},{8,4},{9,5},{1... | collective-permute-start | bytes 393224 | tf_op jit(solution)/shard_map/ppermute | solution.py:27
  151.1 40.2 %copy-start.39 = (f32[128,1,256]{2,0,1:T(8,128)}, f32[128,1,256]{2,0,1:T(8,128)S(1)}, u32[]{:S(2)}) copy-start(f32[128,1,256]{2,0,1:T(8,128)S(1)} %copy.243) | copy-start | bytes 393220
  151.1 11.0 %collective-permute-start.12 = (f32[1,128,256]{2,1,0:T(8,128)S(1)}, f32[1,128,256]{2,1,0:T(8,128)S(1)}, u32[]{:S(2)}, u32[]{:S(2)}) collective-permute-start(f32[1,128,256]{2,1,0:T(8,128)S(1)} %bitcast.569), channel_id=1, source_target_pairs={{0,16},{16,0},{1,17},{17,1},{2,18},{18,2},{3,19},{19,3},{4,20},{20... | collective-permute-start | bytes 393224 | tf_op jit(solution)/shard_map/ppermute | solution.py:16
  152.3 30.9 %copy-start.44 = (f32[128,1,256]{2,0,1:T(8,128)}, f32[128,1,256]{2,0,1:T(8,128)S(1)}, u32[]{:S(2)}) copy-start(f32[128,1,256]{2,0,1:T(8,128)S(1)} %copy.242) | copy-start | bytes 393220
  152.3 17.9 %collective-permute-start.13 = (f32[1,128,256]{2,1,0:T(8,128)S(1)}, f32[1,128,256]{2,1,0:T(8,128)}, u32[]{:S(2)}, u32[]{:S(2)}) collective-permute-start(f32[1,128,256]{2,1,0:T(8,128)S(1)} %bitcast.570), channel_id=1, source_target_pairs={{16,0},{0,16},{17,1},{1,17},{18,2},{2,18},{19,3},{3,19},{20,4},{4,... | collective-permute-start | bytes 393224 | tf_op jit(solution)/shard_map/ppermute | solution.py:19
  155.3 40.4 %copy-start.37 = (f32[128,1,256]{2,0,1:T(8,128)}, f32[128,1,256]{2,0,1:T(8,128)S(1)}, u32[]{:S(2)}) copy-start(f32[128,1,256]{2,0,1:T(8,128)S(1)} %copy.245) | copy-start | bytes 393220
  155.3 30.3 %copy-start.71 = (pred[256]{0:T(512)(128)(4,1)S(1)}, pred[256]{0:T(512)(128)(4,1)}, u32[]{:S(2)}) copy-start(pred[256]{0:T(512)(128)(4,1)} %copy-done.70) | copy-start | bytes 772
  155.3 18.9 %collective-permute-start.14 = (f32[1,128,256]{2,1,0:T(8,128)S(1)}, f32[1,128,256]{2,1,0:T(8,128)}, u32[]{:S(2)}, u32[]{:S(2)}) collective-permute-start(f32[1,128,256]{2,1,0:T(8,128)S(1)} %bitcast.567), channel_id=1, source_target_pairs={{0,1},{1,2},{2,3},{3,4},{4,5},{5,6},{6,7},{7,8},{8,9},{9,10},{10,1... | collective-permute-start | bytes 393224 | tf_op jit(solution)/shard_map/ppermute | solution.py:16
  155.5 38.0 %copy-start.38 = (f32[128,1,256]{2,0,1:T(8,128)}, f32[128,1,256]{2,0,1:T(8,128)S(1)}, u32[]{:S(2)}) copy-start(f32[128,1,256]{2,0,1:T(8,128)S(1)} %copy.244) | copy-start | bytes 393220
  155.5 22.7 %collective-permute-start.15 = (f32[1,128,256]{2,1,0:T(8,128)S(1)}, f32[1,128,256]{2,1,0:T(8,128)}, u32[]{:S(2)}, u32[]{:S(2)}) collective-permute-start(f32[1,128,256]{2,1,0:T(8,128)S(1)} %bitcast.568), channel_id=1, source_target_pairs={{1,0},{2,1},{3,2},{4,3},{5,4},{6,5},{7,6},{8,7},{9,8},{10,9},{11,1... | collective-permute-start | bytes 393224 | tf_op jit(solution)/shard_map/ppermute | solution.py:19
  161.0 38.2 %copy-start.31 = (f32[128,1,256]{2,0,1:T(8,128)}, f32[128,1,256]{2,0,1:T(8,128)S(1)}, u32[]{:S(2)}) copy-start(f32[128,1,256]{2,0,1:T(8,128)S(1)} %copy.247) | copy-start | bytes 393220
  161.0 21.3 %collective-permute-start.16 = (f32[128,256]{1,0:T(8,128)S(1)}, f32[128,256]{1,0:T(8,128)}, u32[]{:S(2)}, u32[]{:S(2)}) collective-permute-start(f32[128,256]{1,0:T(8,128)S(1)} %bitcast.565), channel_id=1, source_target_pairs={{0,4},{1,5},{2,6},{3,7},{4,8},{5,9},{6,10},{7,11},{8,12},{9,13},{1... | collective-permute-start | bytes 393224 | tf_op jit(solution)/shard_map/ppermute | solution.py:27
  162.1 35.8 %copy-start.33 = (f32[128,1,256]{2,0,1:T(8,128)}, f32[128,1,256]{2,0,1:T(8,128)S(1)}, u32[]{:S(2)}) copy-start(f32[128,1,256]{2,0,1:T(8,128)S(1)} %copy.246) | copy-start | bytes 393220
  162.1 25.8 %collective-permute-start.17 = (f32[128,256]{1,0:T(8,128)S(1)}, f32[128,256]{1,0:T(8,128)}, u32[]{:S(2)}, u32[]{:S(2)}) collective-permute-start(f32[128,256]{1,0:T(8,128)S(1)} %bitcast.566), channel_id=1, source_target_pairs={{0,12},{1,13},{2,14},{3,15},{4,0},{5,1},{6,2},{7,3},{8,4},{9,5},{1... | collective-permute-start | bytes 393224 | tf_op jit(solution)/shard_map/ppermute | solution.py:27
  205.7 6.5 %collective-permute-start.18 = (f32[1,128,256]{2,1,0:T(8,128)S(1)}, f32[1,128,256]{2,1,0:T(8,128)S(1)}, u32[]{:S(2)}, u32[]{:S(2)}) collective-permute-start(f32[1,128,256]{2,1,0:T(8,128)S(1)} %get-tuple-element.21), channel_id=1, source_target_pairs={{0,16},{16,0},{1,17},{17,1},{2,18},{18,2},{3,19},{19,3},{4,20},{20... | collective-permute-start | bytes 393224 | tf_op jit(solution)/shard_map/ppermute | solution.py:16
  205.8 14.2 %collective-permute-start.19 = (f32[1,128,256]{2,1,0:T(8,128)}, f32[1,128,256]{2,1,0:T(8,128)}, u32[]{:S(2)}, u32[]{:S(2)}) collective-permute-start(f32[1,128,256]{2,1,0:T(8,128)} %get-tuple-element.17), channel_id=1, source_target_pairs={{16,0},{0,16},{17,1},{1,17},{18,2},{2,18},{19,3},{3,19},{20,4},{4,... | collective-permute-start | bytes 393224 | tf_op jit(solution)/shard_map/ppermute | solution.py:19
  207.7 16.3 %collective-permute-start.20 = (f32[1,128,256]{2,1,0:T(8,128)}, f32[1,128,256]{2,1,0:T(8,128)}, u32[]{:S(2)}, u32[]{:S(2)}) collective-permute-start(f32[1,128,256]{2,1,0:T(8,128)} %get-tuple-element.20), channel_id=1, source_target_pairs={{0,1},{1,2},{2,3},{3,4},{4,5},{5,6},{6,7},{7,8},{8,9},{9,10},{10,1... | collective-permute-start | bytes 393224 | tf_op jit(solution)/shard_map/ppermute | solution.py:16
  207.7 20.3 %collective-permute-start.21 = (f32[1,128,256]{2,1,0:T(8,128)}, f32[1,128,256]{2,1,0:T(8,128)}, u32[]{:S(2)}, u32[]{:S(2)}) collective-permute-start(f32[1,128,256]{2,1,0:T(8,128)} %get-tuple-element.18), channel_id=1, source_target_pairs={{1,0},{2,1},{3,2},{4,3},{5,4},{6,5},{7,6},{8,7},{9,8},{10,9},{11,1... | collective-permute-start | bytes 393224 | tf_op jit(solution)/shard_map/ppermute | solution.py:19
  212.2 19.9 %collective-permute-start.22 = (f32[128,256]{1,0:T(8,128)}, f32[128,256]{1,0:T(8,128)}, u32[]{:S(2)}, u32[]{:S(2)}) collective-permute-start(f32[128,256]{1,0:T(8,128)} %get-tuple-element.19), channel_id=1, source_target_pairs={{0,4},{1,5},{2,6},{3,7},{4,8},{5,9},{6,10},{7,11},{8,12},{9,13},{1... | collective-permute-start | bytes 393224 | tf_op jit(solution)/shard_map/ppermute | solution.py:27
  212.2 26.1 %collective-permute-start.23 = (f32[128,256]{1,0:T(8,128)}, f32[128,256]{1,0:T(8,128)}, u32[]{:S(2)}, u32[]{:S(2)}) collective-permute-start(f32[128,256]{1,0:T(8,128)} %get-tuple-element.16), channel_id=1, source_target_pairs={{0,12},{1,13},{2,14},{3,15},{4,0},{5,1},{6,2},{7,3},{8,4},{9,5},{1... | collective-permute-start | bytes 393224 | tf_op jit(solution)/shard_map/ppermute | solution.py:27
  241.6 50.7 %copy-start.46 = (f32[256,128]{0,1:T(8,128)}, f32[256,128]{0,1:T(8,128)S(1)}, u32[]{:S(2)}) copy-start(f32[256,128]{0,1:T(8,128)S(1)} %copy.216) | copy-start | bytes 393220
  253.5 85.2 %copy-start.72 = (f32[3,96]{1,0:T(4,128)S(1)}, f32[3,96]{1,0:T(4,128)}, u32[]{:S(2)}) copy-start(f32[3,96]{1,0:T(4,128)} %param.14) | copy-start | bytes 3460
  296.7 103.6 %copy-start.14 = (f32[128,1,256]{2,0,1:T(8,128)S(1)}, f32[128,1,256]{2,0,1:T(8,128)}, u32[]{:S(2)}) copy-start(f32[128,1,256]{2,0,1:T(8,128)} %copy-done.13) | copy-start | bytes 393220
  338.8 56.0 %copy-start.79 = (f32[128]{0:T(128)S(1)}, f32[128]{0:T(128)}, u32[]{:S(2)}) copy-start(f32[128]{0:T(128)} %get-tuple-element.5) | copy-start | bytes 1540
  383.2 12.3 %collective-permute-start.24 = (f32[1,128,256]{2,1,0:T(8,128)S(1)}, f32[1,128,256]{2,1,0:T(8,128)S(1)}, u32[]{:S(2)}, u32[]{:S(2)}) collective-permute-start(f32[1,128,256]{2,1,0:T(8,128)S(1)} %bitcast.574), channel_id=1, source_target_pairs={{0,16},{16,0},{1,17},{17,1},{2,18},{18,2},{3,19},{19,3},{4,20},{20... | collective-permute-start | bytes 393224 | tf_op jit(solution)/shard_map/ppermute | solution.py:16
  384.5 17.3 %collective-permute-start.25 = (f32[1,128,256]{2,1,0:T(8,128)S(1)}, f32[1,128,256]{2,1,0:T(8,128)}, u32[]{:S(2)}, u32[]{:S(2)}) collective-permute-start(f32[1,128,256]{2,1,0:T(8,128)S(1)} %bitcast.575), channel_id=1, source_target_pairs={{16,0},{0,16},{17,1},{1,17},{18,2},{2,18},{19,3},{3,19},{20,4},{4,... | collective-permute-start | bytes 393224 | tf_op jit(solution)/shard_map/ppermute | solution.py:19
  387.4 17.0 %collective-permute-start.26 = (f32[1,128,256]{2,1,0:T(8,128)S(1)}, f32[1,128,256]{2,1,0:T(8,128)}, u32[]{:S(2)}, u32[]{:S(2)}) collective-permute-start(f32[1,128,256]{2,1,0:T(8,128)S(1)} %bitcast.572), channel_id=1, source_target_pairs={{0,1},{1,2},{2,3},{3,4},{4,5},{5,6},{6,7},{7,8},{8,9},{9,10},{10,1... | collective-permute-start | bytes 393224 | tf_op jit(solution)/shard_map/ppermute | solution.py:16
  388.5 18.4 %collective-permute-start.27 = (f32[1,128,256]{2,1,0:T(8,128)S(1)}, f32[1,128,256]{2,1,0:T(8,128)}, u32[]{:S(2)}, u32[]{:S(2)}) collective-permute-start(f32[1,128,256]{2,1,0:T(8,128)S(1)} %bitcast.573), channel_id=1, source_target_pairs={{1,0},{2,1},{3,2},{4,3},{5,4},{6,5},{7,6},{8,7},{9,8},{10,9},{11,1... | collective-permute-start | bytes 393224 | tf_op jit(solution)/shard_map/ppermute | solution.py:19
  394.0 15.5 %collective-permute-start.28 = (f32[128,256]{1,0:T(8,128)S(1)}, f32[128,256]{1,0:T(8,128)}, u32[]{:S(2)}, u32[]{:S(2)}) collective-permute-start(f32[128,256]{1,0:T(8,128)S(1)} %bitcast.571), channel_id=1, source_target_pairs={{0,4},{1,5},{2,6},{3,7},{4,8},{5,9},{6,10},{7,11},{8,12},{9,13},{1... | collective-permute-start | bytes 393224 | tf_op jit(solution)/shard_map/ppermute | solution.py:27
  395.5 16.5 %collective-permute-start.29 = (f32[128,256]{1,0:T(8,128)}, f32[128,256]{1,0:T(8,128)}, u32[]{:S(2)}, u32[]{:S(2)}) collective-permute-start(f32[128,256]{1,0:T(8,128)} %bitcast.155), channel_id=1, source_target_pairs={{0,12},{1,13},{2,14},{3,15},{4,0},{5,1},{6,2},{7,3},{8,4},{9,5},{1... | collective-permute-start | bytes 393224 | tf_op jit(solution)/shard_map/ppermute | solution.py:27
  (63 other events, 895.0 us)
where the time goes:
time: 434 us; the launch traced here: 432 us
  blocking collectives  199 us (46%)
  local copies, waits for them, and re-layouts  101 us (23%)
  starting transfers between devices  53.7 us (12%)
  other arithmetic  53 us (12%)
  matrix products  23.3 us (5%)
    all_gather x2, blocking collectives, local(): lax.all_gather(own_values, ('cluster', 'sub'), axis=1, tiled=True)  82.9 us
    psum x2, blocking collectives, local(): lax.psum((coarse_local, local_curve), ('cluster', 'sub'))  79.2 us
    gather x60, local copies, waits for them, and re-layouts, assemble(): permuted = jnp.take(received[face_index], slot_maps[face_index], axis=1)  55.5 us
    unnamed x25, other arithmetic  39.7 us
    psum x1, blocking collectives, precond_with_product(): lax.psum(jnp.sum(vector * precond, axis=1), ('cluster', 'sub'))  36.9 us
    ppermute x10, starting transfers between devices, padded(): lax.ppermute(lax.slice_in_dim(block, 0, width, axis=dim), axis, backward)  28.2 us
    unnamed x184, local copies, waits for them, and re-layouts  20.4 us
    ppermute x10, starting transfers between devices, passed_along(): return lax.ppermute(value, axis, pairs)  19.6 us
  transfers between devices with their start and end apart: 30, of which 0 were waited for; matrix products, arithmetic and copies ran while one was open for 20% of the time, Pallas kernels for 0%

commit v1 on v0

--- a/solution.py
+++ b/solution.py
@@ -5,6 +5,11 @@
 
 ITERS = 2
 STRIDE = 4
+
+
+def gather_and_add(block, axis):
+    terms = lax.all_gather(block, axis)
+    return jnp.sum(terms, axis=0)
 
 
 def padded(block, sides, width):
@@ -79,7 +84,7 @@
             vector.astype(jnp.bfloat16), precond_local, preferred_element_type=jnp.float32
         )
         precond = assemble(local_term)
-        product = 0.5 * lax.psum(jnp.sum(vector * precond, axis=1), ("cluster", "sub"))
+        product = 0.5 * gather_and_add(jnp.sum(vector * precond, axis=1), ("cluster", "sub"))
         return (precond, product)
 
     right_side = assemble(local_loads)

time: 434 us -> 469 us (1.081)
  blocking collectives: 199 us -> 232 us
    all_gather x0 -> x2, blocking collectives: none -> 73.2 us  [gather_and_add(): terms = lax.all_gather(block, axis)]
    psum x1 -> x0, blocking collectives: 36.9 us -> none  [precond_with_product(): lax.psum(jnp.sum(vector * precond, axis=1), ('cluster', 'sub'))]
    unnamed x184 -> x182, local copies, waits for them, and re-layouts: 20.4 us -> 20.4 us
  transfers between devices with their start and end apart: 30 -> 30, of which waited for: 0 -> 0; matrix products, arithmetic and copies ran while one was open for 20% -> 18% of each run, Pallas kernels for 0% -> 0%
where the time goes in v1:
time: 469 us; the launch traced here: 467 us
  blocking collectives  232 us (49%)
  local copies, waits for them, and re-layouts  102 us (22%)
  starting transfers between devices  53.8 us (11%)
  other arithmetic  52.6 us (11%)
  matrix products  23.7 us (5%)
    all_gather x2, blocking collectives, local(): lax.all_gather(own_values, ('cluster', 'sub'), axis=1, tiled=True)  83.1 us
    psum x2, blocking collectives, local(): lax.psum((coarse_local, local_curve), ('cluster', 'sub'))  75.7 us
    all_gather x2, blocking collectives, gather_and_add(): terms = lax.all_gather(block, axis)  73.2 us
    gather x60, local copies, waits for them, and re-layouts, assemble(): permuted = jnp.take(received[face_index], slot_maps[face_index], axis=1)  55.4 us
    unnamed x25, other arithmetic  39.8 us
    ppermute x10, starting transfers between devices, padded(): lax.ppermute(lax.slice_in_dim(block, 0, width, axis=dim), axis, backward)  28.1 us
    unnamed x182, local copies, waits for them, and re-layouts  20.4 us
    ppermute x10, starting transfers between devices, passed_along(): return lax.ppermute(value, axis, pairs)  19.9 us
  transfers between devices with their start and end apart: 30, of which 0 were waited for; matrix products, arithmetic and copies ran while one was open for 18% of the time, Pallas kernels for 0%

profile of v1, /device:TPU:0, one launch (start us, length us, event | category | flops | bytes accessed | tf_op | source)
XLA Modules:
  0.0 466.9 jit_solution(3545503340673559215)
XLA Ops:
  2.3 3.0 collective-permute-start
  5.8 4.5 collective-permute-start.3
  12.5 3.6 collective-permute-start.5
  16.1 6.7 %copy.173 = bf16[1,1536,1536]{1,2,0:T(8,128)(2,1)} copy(bf16[1,1536,1536]{2,1,0:T(8,128)(2,1)} %param.12) | data formatting | bytes 9437184 | tf_op args[2]
  33.1 4.0 fusion.6
  37.9 2.0 collective-permute-start.6
  39.9 4.4 collective-permute-start.9
  44.5 3.9 collective-permute-start.11
  60.5 3.8 multiply_reduce_fusion.3
  65.5 37.8 %all-reduce.1 = (f32[128,96]{0,1:T(8,128)S(1)}, f32[128]{0:T(128)}) all-reduce(f32[128,96]{0,1:T(8,128)} %fusion.53, f32[128]{0:T(128)} %get-tuple-element.4), channel_id=1, replica_groups=mesh['cluster'=2,'sub'=16] {'cluster','sub'}, use_global_device_ids=true, to_apply=%region_4.6 | all-reduce | flops 12416 | bytes 99328 | tf_op jit(solution)/shard_map/psum | solution.py:101
  104.1 41.4 %all-gather.3 = f32[32,3,128]{2,1,0:T(4,128)S(1)} all-gather(f32[1,3,128]{2,1,0:T(4,128)S(1)} %convolution_bitcast_fusion.1), channel_id=1, replica_groups=mesh['cluster'=2,'sub'=16] {'cluster','sub'}, dimensions={0}, use_global_device_ids=true | all-gather | bytes 50688 | tf_op jit(solution)/shard_map/all_gather | solution.py:103
  147.0 36.9 %all-gather.2 = f32[32,1,128]{2,1,0:T(1,128)S(1)} all-gather(f32[1,1,128]{2,1,0:T(1,128)} %bitcast.602), channel_id=2, replica_groups=mesh['cluster'=2,'sub'=16] {'cluster','sub'}, dimensions={0}, use_global_device_ids=true | all-gather | bytes 16896 | tf_op jit(solution)/shard_map/all_gather | solution.py:11
  189.4 2.1 collective-permute-start.13
  192.6 4.5 collective-permute-start.15
  199.3 4.0 collective-permute-start.17
  205.7 1.7 copy.190
  213.7 1.7 copy.196
  222.8 2.3 constant_dynamic-update-slice_fusion.17
  228.5 2.3 constant_dynamic-update-slice_fusion.16
  230.8 2.2 constant_dynamic-update-slice_fusion.15
  233.0 2.2 constant_dynamic-update-slice_fusion.14
  237.7 4.3 fusion.4
  242.8 2.0 collective-permute-start.19
  244.8 4.4 collective-permute-start.21
  249.2 3.8 collective-permute-start.23
  255.4 1.7 copy.206
  259.4 1.7 copy.208
  263.4 1.7 copy.210
  271.4 1.7 copy.214
  273.1 2.2 constant_dynamic-update-slice_fusion.23
  278.7 2.3 constant_dynamic-update-slice_fusion.22
  281.0 2.2 constant_dynamic-update-slice_fusion.21
  283.2 2.2 constant_dynamic-update-slice_fusion.20
  285.4 2.1 constant_dynamic-update-slice_fusion.19
  288.7 1.7 multiply_reduce_fusion.1
  290.4 36.4 %all-gather.4 = f32[32,1,128]{2,1,0:T(1,128)S(1)} all-gather(f32[1,1,128]{2,1,0:T(1,128)S(1)} %bitcast.601), channel_id=3, replica_groups=mesh['cluster'=2,'sub'=16] {'cluster','sub'}, dimensions={0}, use_global_device_ids=true | all-gather | bytes 16896 | tf_op jit(solution)/shard_map/all_gather | solution.py:11
  328.8 4.3 multiply_reduce_fusion
  334.0 37.9 %all-reduce = (f32[128]{0:T(128)}, f32[128,96]{0,1:T(8,128)S(1)}) all-reduce(f32[128]{0:T(128)} %get-tuple-element.84, f32[128,96]{0,1:T(8,128)S(1)} %fusion.52), channel_id=1, replica_groups=mesh['cluster'=2,'sub'=16] {'cluster','sub'}, use_global_device_ids=true, to_apply=%region_9.11 | all-reduce | flops 12416 | bytes 99328 | tf_op jit(solution)/shard_map/psum | solution.py:101
  372.1 41.6 %all-gather.5 = f32[32,3,128]{2,1,0:T(4,128)S(1)} all-gather(f32[1,3,128]{2,1,0:T(4,128)S(1)} %convolution_bitcast_fusion), channel_id=1, replica_groups=mesh['cluster'=2,'sub'=16] {'cluster','sub'}, dimensions={0}, use_global_device_ids=true | all-gather | bytes 50688 | tf_op jit(solution)/shard_map/all_gather | solution.py:103
  418.5 1.7 collective-permute-start.25
  422.2 4.5 collective-permute-start.27
  429.2 4.1 collective-permute-start.29
  449.3 1.7 copy.235
  451.0 2.8 bitcast_dynamic-update-slice_fusion.10
  453.9 2.7 bitcast_dynamic-update-slice_fusion.9
  456.6 2.7 bitcast_dynamic-update-slice_fusion.8
  459.3 2.3 bitcast_dynamic-update-slice_fusion.7
  463.1 3.8 multiply_subtract_fusion
  (374 shorter events, 109.4 us)
Async XLA Ops:
  0.6 63.7 %copy-start = (bf16[1,1536,24]{1,2,0:T(8,128)(2,1)S(1)}, bf16[1,1536,24]{1,2,0:T(8,128)(2,1)}, u32[]{:S(2)}) copy-start(bf16[1,1536,24]{1,2,0:T(8,128)(2,1)} %param.13) | copy-start | bytes 221188
  2.3 10.2 %collective-permute-start = (f32[1,128,256]{2,1,0:T(8,128)S(1)}, f32[1,128,256]{2,1,0:T(8,128)S(1)}, u32[]{:S(2)}, u32[]{:S(2)}) collective-permute-start(f32[1,128,256]{2,1,0:T(8,128)S(1)} %bitcast.565), channel_id=1, source_target_pairs={{0,16},{16,0},{1,17},{17,1},{2,18},{18,2},{3,19},{19,3},{4,20},{20... | collective-permute-start | bytes 393224 | tf_op jit(solution)/shard_map/ppermute | solution.py:21
  5.4 19.0 %collective-permute-start.1 = (f32[1,128,256]{2,1,0:T(8,128)S(1)}, f32[1,128,256]{2,1,0:T(8,128)S(1)}, u32[]{:S(2)}, u32[]{:S(2)}) collective-permute-start(f32[1,128,256]{2,1,0:T(8,128)S(1)} %bitcast.566), channel_id=1, source_target_pairs={{16,0},{0,16},{17,1},{1,17},{18,2},{2,18},{19,3},{3,19},{20,4},{4,... | collective-permute-start | bytes 393224 | tf_op jit(solution)/shard_map/ppermute | solution.py:24
  5.6 19.7 %collective-permute-start.2 = (f32[1,128,256]{2,1,0:T(8,128)S(1)}, f32[1,128,256]{2,1,0:T(8,128)S(1)}, u32[]{:S(2)}, u32[]{:S(2)}) collective-permute-start(f32[1,128,256]{2,1,0:T(8,128)S(1)} %bitcast.562), channel_id=1, source_target_pairs={{0,1},{1,2},{2,3},{3,4},{4,5},{5,6},{6,7},{7,8},{8,9},{9,10},{10,1... | collective-permute-start | bytes 393224 | tf_op jit(solution)/shard_map/ppermute | solution.py:21
  5.8 20.5 %collective-permute-start.3 = (f32[1,128,256]{2,1,0:T(8,128)S(1)}, f32[1,128,256]{2,1,0:T(8,128)S(1)}, u32[]{:S(2)}, u32[]{:S(2)}) collective-permute-start(f32[1,128,256]{2,1,0:T(8,128)S(1)} %bitcast.563), channel_id=1, source_target_pairs={{1,0},{2,1},{3,2},{4,3},{5,4},{6,5},{7,6},{8,7},{9,8},{10,9},{11,1... | collective-permute-start | bytes 393224 | tf_op jit(solution)/shard_map/ppermute | solution.py:24
  10.4 16.9 %collective-permute-start.4 = (f32[128,256]{1,0:T(8,128)S(1)}, f32[128,256]{1,0:T(8,128)S(1)}, u32[]{:S(2)}, u32[]{:S(2)}) collective-permute-start(f32[128,256]{1,0:T(8,128)S(1)} %bitcast.561), channel_id=1, source_target_pairs={{0,4},{1,5},{2,6},{3,7},{4,8},{5,9},{6,10},{7,11},{8,12},{9,13},{1... | collective-permute-start | bytes 393224 | tf_op jit(solution)/shard_map/ppermute | solution.py:32
  11.5 41.7 %copy-start.71 = (pred[256]{0:T(512)(128)(4,1)}, pred[256]{0:T(512)(128)(4,1)S(1)}, u32[]{:S(2)}) copy-start(pred[256]{0:T(512)(128)(4,1)S(1)} %compare_and_fusion.5) | copy-start | bytes 772
  11.5 45.7 %copy-start.69 = (pred[256]{0:T(512)(128)(4,1)}, pred[256]{0:T(512)(128)(4,1)S(1)}, u32[]{:S(2)}) copy-start(pred[256]{0:T(512)(128)(4,1)S(1)} %compare_and_fusion.4) | copy-start | bytes 772
  11.6 46.4 %copy-start.67 = (pred[256]{0:T(512)(128)(4,1)}, pred[256]{0:T(512)(128)(4,1)S(1)}, u32[]{:S(2)}) copy-start(pred[256]{0:T(512)(128)(4,1)S(1)} %compare_and_fusion.3) | copy-start | bytes 772
  11.6 47.0 %copy-start.65 = (pred[256]{0:T(512)(128)(4,1)}, pred[256]{0:T(512)(128)(4,1)S(1)}, u32[]{:S(2)}) copy-start(pred[256]{0:T(512)(128)(4,1)S(1)} %compare_and_fusion.2) | copy-start | bytes 772
  11.6 47.6 %copy-start.63 = (pred[256]{0:T(512)(128)(4,1)}, pred[256]{0:T(512)(128)(4,1)S(1)}, u32[]{:S(2)}) copy-start(pred[256]{0:T(512)(128)(4,1)S(1)} %compare_and_fusion.1) | copy-start | bytes 772
  11.7 48.2 %copy-start.61 = (pred[256]{0:T(512)(128)(4,1)}, pred[256]{0:T(512)(128)(4,1)S(1)}, u32[]{:S(2)}) copy-start(pred[256]{0:T(512)(128)(4,1)S(1)} %compare_and_fusion) | copy-start | bytes 772
  12.5 15.7 %collective-permute-start.5 = (f32[128,256]{1,0:T(8,128)S(1)}, f32[128,256]{1,0:T(8,128)S(1)}, u32[]{:S(2)}, u32[]{:S(2)}) collective-permute-start(f32[128,256]{1,0:T(8,128)S(1)} %bitcast.564), channel_id=1, source_target_pairs={{0,12},{1,13},{2,14},{3,15},{4,0},{5,1},{6,2},{7,3},{8,4},{9,5},{1... | collective-permute-start | bytes 393224 | tf_op jit(solution)/shard_map/ppermute | solution.py:32
  37.9 6.6 %collective-permute-start.6 = (f32[1,128,256]{2,1,0:T(8,128)S(1)}, f32[1,128,256]{2,1,0:T(8,128)S(1)}, u32[]{:S(2)}, u32[]{:S(2)}) collective-permute-start(f32[1,128,256]{2,1,0:T(8,128)S(1)} %get-tuple-element.32), channel_id=1, source_target_pairs={{0,16},{16,0},{1,17},{17,1},{2,18},{18,2},{3,19},{19,3},{4,20},{20... | collective-permute-start | bytes 393224 | tf_op jit(solution)/shard_map/ppermute | solution.py:21
  39.9 9.5 %collective-permute-start.7 = (f32[1,128,256]{2,1,0:T(8,128)S(1)}, f32[1,128,256]{2,1,0:T(8,128)S(1)}, u32[]{:S(2)}, u32[]{:S(2)}) collective-permute-start(f32[1,128,256]{2,1,0:T(8,128)S(1)} %get-tuple-element.28), channel_id=1, source_target_pairs={{16,0},{0,16},{17,1},{1,17},{18,2},{2,18},{19,3},{3,19},{20,4},{4,... | collective-permute-start | bytes 393224 | tf_op jit(solution)/shard_map/ppermute | solution.py:24
  39.9 10.4 %collective-permute-start.8 = (f32[1,128,256]{2,1,0:T(8,128)S(1)}, f32[1,128,256]{2,1,0:T(8,128)S(1)}, u32[]{:S(2)}, u32[]{:S(2)}) collective-permute-start(f32[1,128,256]{2,1,0:T(8,128)S(1)} %get-tuple-element.31), channel_id=1, source_target_pairs={{0,1},{1,2},{2,3},{3,4},{4,5},{5,6},{6,7},{7,8},{8,9},{9,10},{10,1... | collective-permute-start | bytes 393224 | tf_op jit(solution)/shard_map/ppermute | solution.py:21
  39.9 11.3 %collective-permute-start.9 = (f32[1,128,256]{2,1,0:T(8,128)S(1)}, f32[1,128,256]{2,1,0:T(8,128)S(1)}, u32[]{:S(2)}, u32[]{:S(2)}) collective-permute-start(f32[1,128,256]{2,1,0:T(8,128)S(1)} %get-tuple-element.29), channel_id=1, source_target_pairs={{1,0},{2,1},{3,2},{4,3},{5,4},{6,5},{7,6},{8,7},{9,8},{10,9},{11,1... | collective-permute-start | bytes 393224 | tf_op jit(solution)/shard_map/ppermute | solution.py:24
  44.4 7.8 %collective-permute-start.10 = (f32[128,256]{1,0:T(8,128)S(1)}, f32[128,256]{1,0:T(8,128)S(1)}, u32[]{:S(2)}, u32[]{:S(2)}) collective-permute-start(f32[128,256]{1,0:T(8,128)S(1)} %get-tuple-element.30), channel_id=1, source_target_pairs={{0,4},{1,5},{2,6},{3,7},{4,8},{5,9},{6,10},{7,11},{8,12},{9,13},{1... | collective-permute-start | bytes 393224 | tf_op jit(solution)/shard_map/ppermute | solution.py:32
  44.5 9.3 %collective-permute-start.11 = (f32[128,256]{1,0:T(8,128)}, f32[128,256]{1,0:T(8,128)}, u32[]{:S(2)}, u32[]{:S(2)}) collective-permute-start(f32[128,256]{1,0:T(8,128)} %get-tuple-element.27), channel_id=1, source_target_pairs={{0,12},{1,13},{2,14},{3,15},{4,0},{5,1},{6,2},{7,3},{8,4},{9,5},{1... | collective-permute-start | bytes 393224 | tf_op jit(solution)/shard_map/ppermute | solution.py:32
  146.2 53.1 %copy-start.74 = (f32[128]{0:T(128)S(1)}, f32[128]{0:T(128)}, u32[]{:S(2)}) copy-start(f32[128]{0:T(128)} %fusion.51) | copy-start | bytes 1540
  146.2 53.1 %copy-start.77 = (f32[128]{0:T(128)S(1)}, f32[128]{0:T(128)}, u32[]{:S(2)}) copy-start(f32[128]{0:T(128)} %get-tuple-element.8) | copy-start | bytes 1540
  188.3 40.2 %copy-start.39 = (f32[128,1,256]{2,0,1:T(8,128)}, f32[128,1,256]{2,0,1:T(8,128)S(1)}, u32[]{:S(2)}) copy-start(f32[128,1,256]{2,0,1:T(8,128)S(1)} %copy.243) | copy-start | bytes 393220
  188.3 11.0 %collective-permute-start.12 = (f32[1,128,256]{2,1,0:T(8,128)S(1)}, f32[1,128,256]{2,1,0:T(8,128)S(1)}, u32[]{:S(2)}, u32[]{:S(2)}) collective-permute-start(f32[1,128,256]{2,1,0:T(8,128)S(1)} %bitcast.571), channel_id=1, source_target_pairs={{0,16},{16,0},{1,17},{17,1},{2,18},{18,2},{3,19},{19,3},{4,20},{20... | collective-permute-start | bytes 393224 | tf_op jit(solution)/shard_map/ppermute | solution.py:21
  189.4 18.0 %collective-permute-start.13 = (f32[1,128,256]{2,1,0:T(8,128)S(1)}, f32[1,128,256]{2,1,0:T(8,128)}, u32[]{:S(2)}, u32[]{:S(2)}) collective-permute-start(f32[1,128,256]{2,1,0:T(8,128)S(1)} %bitcast.572), channel_id=1, source_target_pairs={{16,0},{0,16},{17,1},{1,17},{18,2},{2,18},{19,3},{3,19},{20,4},{4,... | collective-permute-start | bytes 393224 | tf_op jit(solution)/shard_map/ppermute | solution.py:24
  192.4 40.5 %copy-start.37 = (f32[128,1,256]{2,0,1:T(8,128)}, f32[128,1,256]{2,0,1:T(8,128)S(1)}, u32[]{:S(2)}) copy-start(f32[128,1,256]{2,0,1:T(8,128)S(1)} %copy.245) | copy-start | bytes 393220
  192.5 18.9 %collective-permute-start.14 = (f32[1,128,256]{2,1,0:T(8,128)S(1)}, f32[1,128,256]{2,1,0:T(8,128)}, u32[]{:S(2)}, u32[]{:S(2)}) collective-permute-start(f32[1,128,256]{2,1,0:T(8,128)S(1)} %bitcast.569), channel_id=1, source_target_pairs={{0,1},{1,2},{2,3},{3,4},{4,5},{5,6},{6,7},{7,8},{8,9},{9,10},{10,1... | collective-permute-start | bytes 393224 | tf_op jit(solution)/shard_map/ppermute | solution.py:21
  192.6 38.1 %copy-start.38 = (f32[128,1,256]{2,0,1:T(8,128)}, f32[128,1,256]{2,0,1:T(8,128)S(1)}, u32[]{:S(2)}) copy-start(f32[128,1,256]{2,0,1:T(8,128)S(1)} %copy.244) | copy-start | bytes 393220
  192.6 22.8 %collective-permute-start.15 = (f32[1,128,256]{2,1,0:T(8,128)S(1)}, f32[1,128,256]{2,1,0:T(8,128)}, u32[]{:S(2)}, u32[]{:S(2)}) collective-permute-start(f32[1,128,256]{2,1,0:T(8,128)S(1)} %bitcast.570), channel_id=1, source_target_pairs={{1,0},{2,1},{3,2},{4,3},{5,4},{6,5},{7,6},{8,7},{9,8},{10,9},{11,1... | collective-permute-start | bytes 393224 | tf_op jit(solution)/shard_map/ppermute | solution.py:24
  198.1 38.3 %copy-start.31 = (f32[128,1,256]{2,0,1:T(8,128)}, f32[128,1,256]{2,0,1:T(8,128)S(1)}, u32[]{:S(2)}) copy-start(f32[128,1,256]{2,0,1:T(8,128)S(1)} %copy.247) | copy-start | bytes 393220
  198.1 21.3 %collective-permute-start.16 = (f32[128,256]{1,0:T(8,128)S(1)}, f32[128,256]{1,0:T(8,128)}, u32[]{:S(2)}, u32[]{:S(2)}) collective-permute-start(f32[128,256]{1,0:T(8,128)S(1)} %bitcast.567), channel_id=1, source_target_pairs={{0,4},{1,5},{2,6},{3,7},{4,8},{5,9},{6,10},{7,11},{8,12},{9,13},{1... | collective-permute-start | bytes 393224 | tf_op jit(solution)/shard_map/ppermute | solution.py:32
  199.2 35.9 %copy-start.33 = (f32[128,1,256]{2,0,1:T(8,128)}, f32[128,1,256]{2,0,1:T(8,128)S(1)}, u32[]{:S(2)}) copy-start(f32[128,1,256]{2,0,1:T(8,128)S(1)} %copy.246) | copy-start | bytes 393220
  199.3 25.8 %collective-permute-start.17 = (f32[128,256]{1,0:T(8,128)S(1)}, f32[128,256]{1,0:T(8,128)}, u32[]{:S(2)}, u32[]{:S(2)}) collective-permute-start(f32[128,256]{1,0:T(8,128)S(1)} %bitcast.568), channel_id=1, source_target_pairs={{0,12},{1,13},{2,14},{3,15},{4,0},{5,1},{6,2},{7,3},{8,4},{9,5},{1... | collective-permute-start | bytes 393224 | tf_op jit(solution)/shard_map/ppermute | solution.py:32
  242.8 6.5 %collective-permute-start.18 = (f32[1,128,256]{2,1,0:T(8,128)S(1)}, f32[1,128,256]{2,1,0:T(8,128)S(1)}, u32[]{:S(2)}, u32[]{:S(2)}) collective-permute-start(f32[1,128,256]{2,1,0:T(8,128)S(1)} %get-tuple-element.20), channel_id=1, source_target_pairs={{0,16},{16,0},{1,17},{17,1},{2,18},{18,2},{3,19},{19,3},{4,20},{20... | collective-permute-start | bytes 393224 | tf_op jit(solution)/shard_map/ppermute | solution.py:21
  242.8 14.3 %collective-permute-start.19 = (f32[1,128,256]{2,1,0:T(8,128)}, f32[1,128,256]{2,1,0:T(8,128)}, u32[]{:S(2)}, u32[]{:S(2)}) collective-permute-start(f32[1,128,256]{2,1,0:T(8,128)} %get-tuple-element.16), channel_id=1, source_target_pairs={{16,0},{0,16},{17,1},{1,17},{18,2},{2,18},{19,3},{3,19},{20,4},{4,... | collective-permute-start | bytes 393224 | tf_op jit(solution)/shard_map/ppermute | solution.py:24
  244.8 16.3 %collective-permute-start.20 = (f32[1,128,256]{2,1,0:T(8,128)}, f32[1,128,256]{2,1,0:T(8,128)}, u32[]{:S(2)}, u32[]{:S(2)}) collective-permute-start(f32[1,128,256]{2,1,0:T(8,128)} %get-tuple-element.19), channel_id=1, source_target_pairs={{0,1},{1,2},{2,3},{3,4},{4,5},{5,6},{6,7},{7,8},{8,9},{9,10},{10,1... | collective-permute-start | bytes 393224 | tf_op jit(solution)/shard_map/ppermute | solution.py:21
  244.8 20.3 %collective-permute-start.21 = (f32[1,128,256]{2,1,0:T(8,128)}, f32[1,128,256]{2,1,0:T(8,128)}, u32[]{:S(2)}, u32[]{:S(2)}) collective-permute-start(f32[1,128,256]{2,1,0:T(8,128)} %get-tuple-element.17), channel_id=1, source_target_pairs={{1,0},{2,1},{3,2},{4,3},{5,4},{6,5},{7,6},{8,7},{9,8},{10,9},{11,1... | collective-permute-start | bytes 393224 | tf_op jit(solution)/shard_map/ppermute | solution.py:24
  249.2 19.9 %collective-permute-start.22 = (f32[128,256]{1,0:T(8,128)}, f32[128,256]{1,0:T(8,128)}, u32[]{:S(2)}, u32[]{:S(2)}) collective-permute-start(f32[128,256]{1,0:T(8,128)} %get-tuple-element.18), channel_id=1, source_target_pairs={{0,4},{1,5},{2,6},{3,7},{4,8},{5,9},{6,10},{7,11},{8,12},{9,13},{1... | collective-permute-start | bytes 393224 | tf_op jit(solution)/shard_map/ppermute | solution.py:32
  249.2 26.1 %collective-permute-start.23 = (f32[128,256]{1,0:T(8,128)}, f32[128,256]{1,0:T(8,128)}, u32[]{:S(2)}, u32[]{:S(2)}) collective-permute-start(f32[128,256]{1,0:T(8,128)} %get-tuple-element.15), channel_id=1, source_target_pairs={{0,12},{1,13},{2,14},{3,15},{4,0},{5,1},{6,2},{7,3},{8,4},{9,5},{1... | collective-permute-start | bytes 393224 | tf_op jit(solution)/shard_map/ppermute | solution.py:32
  278.7 50.1 %copy-start.46 = (f32[256,128]{0,1:T(8,128)}, f32[256,128]{0,1:T(8,128)S(1)}, u32[]{:S(2)}) copy-start(f32[256,128]{0,1:T(8,128)S(1)} %copy.216) | copy-start | bytes 393220
  290.4 81.5 %copy-start.73 = (f32[3,96]{1,0:T(4,128)S(1)}, f32[3,96]{1,0:T(4,128)}, u32[]{:S(2)}) copy-start(f32[3,96]{1,0:T(4,128)} %param.14) | copy-start | bytes 3460
  333.1 102.0 %copy-start.14 = (f32[128,1,256]{2,0,1:T(8,128)S(1)}, f32[128,1,256]{2,0,1:T(8,128)}, u32[]{:S(2)}) copy-start(f32[128,1,256]{2,0,1:T(8,128)} %copy-done.13) | copy-start | bytes 393220
  372.1 56.5 %copy-start.78 = (f32[128]{0:T(128)S(1)}, f32[128]{0:T(128)}, u32[]{:S(2)}) copy-start(f32[128]{0:T(128)} %get-tuple-element.5) | copy-start | bytes 1540
  417.0 12.2 %collective-permute-start.24 = (f32[1,128,256]{2,1,0:T(8,128)S(1)}, f32[1,128,256]{2,1,0:T(8,128)S(1)}, u32[]{:S(2)}, u32[]{:S(2)}) collective-permute-start(f32[1,128,256]{2,1,0:T(8,128)S(1)} %bitcast.576), channel_id=1, source_target_pairs={{0,16},{16,0},{1,17},{17,1},{2,18},{18,2},{3,19},{19,3},{4,20},{20... | collective-permute-start | bytes 393224 | tf_op jit(solution)/shard_map/ppermute | solution.py:21
  418.5 18.3 %collective-permute-start.25 = (f32[1,128,256]{2,1,0:T(8,128)S(1)}, f32[1,128,256]{2,1,0:T(8,128)}, u32[]{:S(2)}, u32[]{:S(2)}) collective-permute-start(f32[1,128,256]{2,1,0:T(8,128)S(1)} %bitcast.577), channel_id=1, source_target_pairs={{16,0},{0,16},{17,1},{1,17},{18,2},{2,18},{19,3},{3,19},{20,4},{4,... | collective-permute-start | bytes 393224 | tf_op jit(solution)/shard_map/ppermute | solution.py:24
  421.2 18.1 %collective-permute-start.26 = (f32[1,128,256]{2,1,0:T(8,128)S(1)}, f32[1,128,256]{2,1,0:T(8,128)}, u32[]{:S(2)}, u32[]{:S(2)}) collective-permute-start(f32[1,128,256]{2,1,0:T(8,128)S(1)} %bitcast.574), channel_id=1, source_target_pairs={{0,1},{1,2},{2,3},{3,4},{4,5},{5,6},{6,7},{7,8},{8,9},{9,10},{10,1... | collective-permute-start | bytes 393224 | tf_op jit(solution)/shard_map/ppermute | solution.py:21
  422.2 19.6 %collective-permute-start.27 = (f32[1,128,256]{2,1,0:T(8,128)S(1)}, f32[1,128,256]{2,1,0:T(8,128)}, u32[]{:S(2)}, u32[]{:S(2)}) collective-permute-start(f32[1,128,256]{2,1,0:T(8,128)S(1)} %bitcast.575), channel_id=1, source_target_pairs={{1,0},{2,1},{3,2},{4,3},{5,4},{6,5},{7,6},{8,7},{9,8},{10,9},{11,1... | collective-permute-start | bytes 393224 | tf_op jit(solution)/shard_map/ppermute | solution.py:24
  427.7 16.6 %collective-permute-start.28 = (f32[128,256]{1,0:T(8,128)S(1)}, f32[128,256]{1,0:T(8,128)}, u32[]{:S(2)}, u32[]{:S(2)}) collective-permute-start(f32[128,256]{1,0:T(8,128)S(1)} %bitcast.573), channel_id=1, source_target_pairs={{0,4},{1,5},{2,6},{3,7},{4,8},{5,9},{6,10},{7,11},{8,12},{9,13},{1... | collective-permute-start | bytes 393224 | tf_op jit(solution)/shard_map/ppermute | solution.py:32
  429.2 17.7 %collective-permute-start.29 = (f32[128,256]{1,0:T(8,128)}, f32[128,256]{1,0:T(8,128)}, u32[]{:S(2)}, u32[]{:S(2)}) collective-permute-start(f32[128,256]{1,0:T(8,128)} %bitcast.157), channel_id=1, source_target_pairs={{0,12},{1,13},{2,14},{3,15},{4,0},{5,1},{6,2},{7,3},{8,4},{9,5},{1... | collective-permute-start | bytes 393224 | tf_op jit(solution)/shard_map/ppermute | solution.py:32
  (62 other events, 921.2 us)
